TPU v7x, 32 devices: a whole 2x2x4 slice. The times are simulated.
32 devices in a mesh: space: 8 (over y, x, core), mode: 4 (over z).
Axes of the slice: x: 2, y: 2, z: 4, core: 2. Of those that a mesh axis runs over, the one named last changes fastest.
Arguments:
- modes: bfloat16 [512, 96, 2048], P('mode', 'space'), may hold values from -6 to 6
- phases: int32 [96, 2048], P('space'), may hold values from 0 to 2
- velocity: float32 [3], replicated, may hold values from 0.5 to 1.5
Outputs:
- reduced: float32 [512, 512], P('space', 'mode')
All inputs are finite; a program needn't handle non-finite values.
Results may differ from a plain program's by a relative error of at most 0.0028.
Values may be sent and summed in bfloat16 or wider, within the bound.
No kernel may reach another device: no remote copies, remote signals or barrier semaphores. Data moves between devices by JAX's collectives and lax.ppermute only.
A program may use at most 192 MiB of HBM per device.

v0:
```python
import math
import jax
import jax.numpy as jnp
from jax import lax
from jax.sharding import PartitionSpec as P

NZ = 64


def extended(array, sides, width):
    for axis, dim in sides:
        devices, length = (lax.axis_size(axis), array.shape[dim])
        up = [(i, (i + 1) % devices) for i in range(devices - 1)]
        down = [(j, i) for i, j in up]
        last = lax.slice_in_dim(array, length - width, length, axis=dim)
        initial = lax.slice_in_dim(array, 0, width, axis=dim)
        before = lax.ppermute(last, axis, up)
        after = lax.ppermute(initial, axis, down)
        array = jnp.concatenate([before, array, after], axis=dim)
    return array


def shifted(field, offset):
    width = field.shape[-1]
    zeros_part = jnp.zeros(field.shape[:-1] + (abs(offset),), jnp.float32)
    if offset > 0:
        return jnp.concatenate([field[..., offset:], zeros_part], axis=-1)
    return jnp.concatenate([zeros_part, field[..., : width + offset]], axis=-1)


def inner_rows(left, right):
    left_flat = left.reshape(left.shape[0], -1)
    right_flat = right.reshape(right.shape[0], -1)
    return lax.dot_general(
        left_flat, right_flat, (((1,), (1,)), ((), ())), preferred_element_type=jnp.float32
    )


def local(modes, phases, velocity):
    weight = jnp.where(phases == 0, 0.1, jnp.where(phases == 1, 1.0, 0.5)).astype(jnp.float32)
    total_cells = lax.axis_size("space") * modes.shape[1] * modes.shape[2]
    eps = 1.0 / math.sqrt(total_cells)
    padded = extended(modes, (("space", 1),), 1).astype(jnp.float32)
    center = padded[:, 1:-1]
    x_up = padded[:, 2:]
    x_down = padded[:, :-2]
    zpos = lax.broadcasted_iota(jnp.int32, (1, 1, center.shape[-1]), 2) % NZ
    z_up = jnp.where(zpos == NZ - 1, 0.0, shifted(center, 1))
    z_down = jnp.where(zpos == 0, 0.0, shifted(center, -1))
    y_up = shifted(center, NZ)
    y_down = shifted(center, -NZ)
    spread = x_up + x_down + y_up + y_down + z_up + z_down - 6.0 * center
    drift = (
        velocity[0] * (x_up - x_down)
        + velocity[1] * (y_up - y_down)
        + velocity[2] * (z_up - z_down)
    )
    applied = (weight[None] * (eps * spread - 0.5 * drift)).astype(jnp.bfloat16)
    partial_cols = inner_rows(lax.all_gather(modes, "mode", axis=0, tiled=True), applied)
    summed = lax.psum_scatter(partial_cols, "space", scatter_dimension=0, tiled=True)
    return summed * eps


def solution(mesh):
    placed = (P("mode", "space", None), P("space", None), P())
    return jax.shard_map(
        local, mesh=mesh, in_specs=placed, out_specs=P("space", "mode"), check_vma=False
    )
```

profile of v0, /device:TPU:0, one launch (start us, length us, event | category | flops | bytes accessed | tf_op | source)
XLA Modules:
  0.0 492.9 jit_solution(3091800072277738935)
XLA Ops:
  6.5 0.0 all-gather.2.cloned.1.call-start
  6.5 0.7 all-gather.2.cloned.1.call-update
  7.3 0.0 reduce-scatter.4.cloned.1.call-start
  7.3 1.3 fusion.21
  8.6 2.4 collective-permute-start
  11.0 1.3 collective-permute-start.1
  12.3 1.4 fusion.22
  13.6 0.9 select_select_fusion
  14.6 0.0 collective-permute-done
  14.6 2.3 collective-permute-done.1
  16.9 12.4 %maximum_convert_fusion = f32[128,14,2048]{2,0,1:T(8,128)} fusion(bf16[128,1,2048]{2,0,1:T(8,128)(2,1)S(1)} %collective-permute-done.1, bf16[128,12,2048]{2,0,1:T(8,128)(2,1)} %param.3, bf16[128,1,2048]{2,0,1:T(8,128)(2,1)S(1)} %collective-permute-done), kind=kLoop, calls=%fused_computation.6 | loop fusion | flops 11010048 | bytes 22020096 | tf_op jit(solution)/shard_map/convert_element_type | solution.py:43
  29.2 0.0 copy-start
  29.2 22.5 %fusion.19 = (f32[128,12,1984]{2,0,1:T(8,128)}, f32[128,12,1984]{2,0,1:T(8,128)}) fusion(f32[128,14,2048]{2,0,1:T(8,128)} %maximum_convert_fusion), kind=kLoop, calls=%fused_computation.22 | loop fusion | bytes 48758784 | tf_op jit(solution)/shard_map/slice | solution.py:27
  51.7 0.0 copy-done
  51.7 10.0 %fusion.20 = (f32[128,12,2047]{2,0,1:T(8,128)}, f32[128,12,2047]{2,0,1:T(8,128)}) fusion(f32[128,14,2048]{2,0,1:T(8,128)S(1)} %copy-done), kind=kLoop, calls=%fused_computation.23 | loop fusion | bytes 50307072 | tf_op jit(solution)/shard_map/slice | solution.py:27
  61.8 34.4 %fusion.27 = bf16[128,12,2048]{2,0,1:T(8,128)(2,1)} fusion(f32[128,14,2048]{2,0,1:T(8,128)} %maximum_convert_fusion, f32[128,12,2047]{2,0,1:T(8,128)} %get-tuple-element.8, f32[128,12,2047]{2,0,1:T(8,128)} %get-tuple-element.7, f32[128,12,1984]{2,0,1:T(8,128)} %get-tuple-element.6, f32[128,12,1984]{2,0,1:T(8,128)} %get-tuple-element.5, ...), kind=kLoop, calls=%fused_computation.5.clone.clone.clone.clone.1 | loop fusion | flops 69206016 | bytes 93675536 | tf_op jit(solution)/shard_map/dot_general | solution.py:34
  96.2 340.7 %all-gather.2.cloned.1.call-done = bf16[512,12,2048]{2,0,1:T(8,128)(2,1)} async-done(((bf16[128,12,2048]{2,0,1:T(8,128)(2,1)}), bf16[512,12,2048]{2,0,1:T(8,128)(2,1)}) %all-gather.2.cloned.1.call-update) | async-done | bytes 25165840 | tf_op jit(solution)/shard_map/all_gather | solution.py:59
  436.8 15.1 %fusion.7 = f32[512,128]{0,1:T(8,128)S(1)} fusion(bf16[512,12,2048]{2,0,1:T(8,128)(2,1)} %all-gather.2.cloned.1.call-done, bf16[128,12,2048]{2,0,1:T(8,128)(2,1)} %fusion.27), kind=kOutput, calls=%fused_computation.8 | convolution fusion | flops 3221225472 | bytes 31719424 | tf_op jit(solution)/shard_map/dot_general | solution.py:34
  451.9 0.8 copy.7
  452.7 0.0 reduce-scatter.4.cloned.1.call-update
  452.8 32.0 %reduce-scatter.4.cloned.1.call-done = f32[64,128]{1,0:T(8,128)} async-done(((f32[512,128]{1,0:T(8,128)}), f32[64,128]{1,0:T(8,128)}) %reduce-scatter.4.cloned.1.call-update) | async-done | bytes 32784 | tf_op jit(solution)/shard_map/reduce_scatter | solution.py:60
  484.7 1.4 broadcast_multiply_fusion
  (1 shorter events, 0.0 us)
Async XLA Ops:
  6.5 430.3 %all-gather.2.cloned.1.call-start = ((), (), s32[]{:S(2)}) async-start(), calls=%async_computation.1 | async-start | bytes 31457280 | tf_op jit(solution)/shard_map/all_gather | solution.py:59
  7.3 477.5 %reduce-scatter.4.cloned.1.call-start = ((), (), s32[]{:S(2)}) async-start(), calls=%async_computation.2 | async-start | bytes 294912 | tf_op jit(solution)/shard_map/reduce_scatter | solution.py:60
  8.6 6.0 %collective-permute-start = (bf16[128,1,2048]{2,0,1:T(8,128)(2,1)S(1)}, bf16[128,1,2048]{2,0,1:T(8,128)(2,1)S(1)}, u32[]{:S(2)}, u32[]{:S(2)}) collective-permute-start(bf16[128,1,2048]{2,0,1:T(8,128)(2,1)S(1)} %get-tuple-element.9), channel_id=1, source_target_pairs={{0,4},{4,8},{8,12},{12,16},{16,20},{20,24},{24,28},{1,5},{5,9},{9,... | collective-permute-start | bytes 1572872 | tf_op jit(solution)/shard_map/ppermute | solution.py:17
  11.0 5.9 %collective-permute-start.1 = (bf16[128,1,2048]{2,0,1:T(8,128)(2,1)S(1)}, bf16[128,1,2048]{2,0,1:T(8,128)(2,1)S(1)}, u32[]{:S(2)}, u32[]{:S(2)}) collective-permute-start(bf16[128,1,2048]{2,0,1:T(8,128)(2,1)S(1)} %get-tuple-element.10), channel_id=1, source_target_pairs={{4,0},{8,4},{12,8},{16,12},{20,16},{24,20},{28,24},{5,1},{9,5},{13... | collective-permute-start | bytes 1572872 | tf_op jit(solution)/shard_map/ppermute | solution.py:18
  29.2 22.5 %copy-start = (f32[128,14,2048]{2,0,1:T(8,128)S(1)}, f32[128,14,2048]{2,0,1:T(8,128)}, u32[]{:S(2)}) copy-start(f32[128,14,2048]{2,0,1:T(8,128)} %maximum_convert_fusion) | copy-start | bytes 44040196
Sparse Core Ops, SparseCore 0:
  8.9 427.8 all-gather.1
  452.9 31.7 reduce-scatter.3
where the time goes:
time: 493 us
  waiting for transfers between devices  376 us (76%)
  other arithmetic  49.1 us (10%)
  local copies, waits for them, and re-layouts  36 us (7%)
  matrix products  15.1 us (3%)
  between operations  13.4 us (3%)
    all_gather x1, waiting for transfers between devices, local(): lax.all_gather(modes, 'mode', axis=0, tiled=True)  341 us
    dot_general x1, other arithmetic, inner_rows(): lax.dot_general(left_flat, right_flat, (((1,), (1,)), ((), ())), preferre...  34.4 us
    slice x2, local copies, waits for them, and re-layouts, shifted(): return jnp.concatenate([field[..., offset:], zeros_part], axis=-1)  32.5 us
    reduce_scatter x1, waiting for transfers between devices, local(): lax.psum_scatter(partial_cols, 'space', scatter_dimension=0, tiled=True)  32 us
    dot_general x1, matrix products, inner_rows(): lax.dot_general(left_flat, right_flat, (((1,), (1,)), ((), ())), preferre...  15.1 us
    convert_element_type x1, other arithmetic, local(): padded = extended(modes, (('space', 1),), 1).astype(jnp.float32)  12.4 us
  transfers between devices with their start and end apart: 4, of which 3 were waited for; matrix products, arithmetic and copies ran while one was open for 17% of the time, Pallas kernels for 0%

commit v1 on v0

--- a/solution.py
+++ b/solution.py
@@ -5,6 +5,28 @@
 from jax.sharding import PartitionSpec as P
 
 NZ = 64
+
+
+def joined_along(blocks, dim):
+    shape = list(blocks.shape[1:])
+    shape[dim] *= blocks.shape[0]
+    return jnp.moveaxis(blocks, 0, dim).reshape(shape)
+
+
+def ring_gather(array, axis, dim):
+    size = lax.axis_size(axis)
+    pairs = [(i, (i + 1) % size) for i in range(size)]
+    back = [(b, a) for a, b in pairs]
+    lower, upper = ([], [])
+    for lap in range(size - 1):
+        if lap % 2 == 0:
+            lower.append(lax.ppermute(lower[-1] if lower else array, axis, pairs))
+        else:
+            upper.append(lax.ppermute(upper[-1] if upper else array, axis, back))
+    parts = jnp.stack([*lower[::-1], array, *upper])
+    shift = lax.axis_index(axis) - len(lower)
+    parts = parts[(jnp.arange(size) - shift) % size]
+    return joined_along(parts, dim)
 
 
 def extended(array, sides, width):
@@ -56,7 +78,7 @@
         + velocity[2] * (z_up - z_down)
     )
     applied = (weight[None] * (eps * spread - 0.5 * drift)).astype(jnp.bfloat16)
-    partial_cols = inner_rows(lax.all_gather(modes, "mode", axis=0, tiled=True), applied)
+    partial_cols = inner_rows(ring_gather(modes, "mode", 0), applied)
     summed = lax.psum_scatter(partial_cols, "space", scatter_dimension=0, tiled=True)
     return summed * eps
 

time: 493 us -> 596 us (1.21)
  local copies, waits for them, and re-layouts: 36 us -> 123 us
  other arithmetic: 49.1 us -> 70.7 us
  waiting for transfers between devices: 376 us -> 363 us
    all_gather x1 -> x0, waiting for transfers between devices: 341 us -> none  [local(): lax.all_gather(modes, 'mode', axis=0, tiled=True)]
    ppermute x0 -> x3, waiting for transfers between devices: none -> 329 us  [the longest x2 258 us: ring_gather(): lower.append(lax.ppermute(lower[-1] if lower else array, axis, pairs))]
    unnamed x3 -> x12, local copies, waits for them, and re-layouts: 0.84 us -> 47.4 us
    gather x0 -> x5, local copies, waits for them, and re-layouts: none -> 44.3 us  [ring_gather(): parts = parts[(jnp.arange(size) - shift) % size]]
    dot_general x1 -> x0, other arithmetic: 34.4 us -> none  [inner_rows(): lax.dot_general(left_flat, right_flat, (((1,), (1,)), ((), ())), preferre...]
    convert_element_type x0 -> x1, other arithmetic: none -> 23.8 us  [local(): applied = (weight[None] * (eps * spread - 0.5 * drift)).astype(jnp.bfloat16)]
    another operation x0 -> x1, other arithmetic: none -> 18.2 us  [ring_gather(): parts = jnp.stack([*lower[::-1], array, *upper])]
    unnamed x0 -> x2, other arithmetic: none -> 17.4 us
  transfers between devices with their start and end apart: 4 -> 6, of which waited for: 3 -> 4; matrix products, arithmetic and copies ran while one was open for 17% -> 12% of each run, Pallas kernels for 0% -> 0%
where the time goes in v1:
time: 596 us; the launch traced here: 595 us
  waiting for transfers between devices  363 us (61%)
  local copies, waits for them, and re-layouts  123 us (21%)
  other arithmetic  70.7 us (12%)
  matrix products  17.3 us (3%)
  between operations  13.5 us (2%)
  starting transfers between devices  7.9 us (1%)
    ppermute x2, waiting for transfers between devices, ring_gather(): lower.append(lax.ppermute(lower[-1] if lower else array, axis, pairs))  258 us
    ppermute x1, waiting for transfers between devices, ring_gather(): upper.append(lax.ppermute(upper[-1] if upper else array, axis, back))  71 us
    unnamed x12, local copies, waits for them, and re-layouts  47.4 us
    gather x5, local copies, waits for them, and re-layouts, ring_gather(): parts = parts[(jnp.arange(size) - shift) % size]  44.3 us
    reduce_scatter x1, waiting for transfers between devices, local(): lax.psum_scatter(partial_cols, 'space', scatter_dimension=0, tiled=True)  33.1 us
    slice x2, local copies, waits for them, and re-layouts, shifted(): return jnp.concatenate([field[..., offset:], zeros_part], axis=-1)  28.9 us
    convert_element_type x1, other arithmetic, local(): applied = (weight[None] * (eps * spread - 0.5 * drift)).astype(jnp.bfloat16)  23.8 us
    another operation x1, other arithmetic, ring_gather(): parts = jnp.stack([*lower[::-1], array, *upper])  18.2 us
  transfers between devices with their start and end apart: 6, of which 4 were waited for; matrix products, arithmetic and copies ran while one was open for 12% of the time, Pallas kernels for 0%

profile of v1, /device:TPU:0, one launch (start us, length us, event | category | flops | bytes accessed | tf_op | source)
XLA Modules:
  0.0 594.5 jit_solution(15472242460411354814)
XLA Ops:
  6.5 0.0 copy-start.2
  6.5 0.0 copy-start.1
  6.5 0.0 reduce-scatter.2.cloned.1.call-start
  6.5 3.0 collective-permute-start
  9.6 2.1 collective-permute-start.2
  11.6 8.6 %copy.5 = bf16[128,12,2048]{0,2,1:T(8,128)(2,1)} copy(bf16[128,12,2048]{2,0,1:T(8,128)(2,1)} %param.3) | data formatting | bytes 12582912 | tf_op args[0]
  20.3 1.3 fusion.18
  21.5 1.5 collective-permute-start.3
  23.0 1.3 collective-permute-start.4
  24.4 0.0 copy-done.2
  24.4 0.6 fusion.19
  25.0 123.3 %collective-permute-done = bf16[128,12,2048]{2,0,1:T(8,128)(2,1)} collective-permute-done((bf16[128,12,2048]{2,0,1:T(8,128)(2,1)}, bf16[128,12,2048]{2,0,1:T(8,128)(2,1)}, u32[]{:S(2)}, u32[]{:S(2)}) %collective-permute-start) | collective-permute-done | bytes 6291488 | tf_op jit(solution)/shard_map/ppermute | solution.py:23
  148.3 0.0 collective-permute-start.1
  148.3 0.0 copy-done.1
  148.3 0.7 select_select_fusion
  149.0 0.0 collective-permute-done.3
  149.0 0.0 collective-permute-done.4
  149.0 9.2 %maximum_convert_fusion = f32[128,14,2048]{0,2,1:T(8,128)} fusion(bf16[128,1,2048]{0,2,1:T(8,128)(2,1)S(1)} %collective-permute-done.4, bf16[128,12,2048]{0,2,1:T(8,128)(2,1)} %copy.5, bf16[128,1,2048]{0,2,1:T(8,128)(2,1)S(1)} %collective-permute-done.3), kind=kLoop, calls=%fused_computation.15 | loop fusion | flops 11010048 | bytes 22020096 | tf_op jit(solution)/shard_map/convert_element_type | solution.py:65
  158.1 0.0 copy-start
  158.1 20.0 %fusion.17 = (f32[128,12,2047]{0,2,1:T(8,128)}, f32[128,12,2047]{0,2,1:T(8,128)}) fusion(f32[128,14,2048]{0,2,1:T(8,128)} %maximum_convert_fusion), kind=kLoop, calls=%fused_computation.34 | loop fusion | bytes 50307072 | tf_op jit(solution)/shard_map/slice | solution.py:49
  178.1 0.0 copy-done
  178.1 0.0 slice-start
  178.1 9.0 %fusion.16 = (f32[128,12,1984]{0,2,1:T(8,128)}, f32[128,12,1984]{0,2,1:T(8,128)}) fusion(f32[128,14,2048]{0,2,1:T(8,128)S(1)} %copy-done), kind=kLoop, calls=%fused_computation.33 | loop fusion | bytes 48758784 | tf_op jit(solution)/shard_map/slice | solution.py:49
  187.1 0.0 slice-start.1
  187.1 23.8 %fusion.7 = bf16[128,12,2048]{0,2,1:T(8,128)(2,1)} fusion(f32[128,14,2048]{0,2,1:T(8,128)S(1)} %copy-done, f32[128,12,2047]{0,2,1:T(8,128)} %get-tuple-element.12, f32[128,12,2047]{0,2,1:T(8,128)} %get-tuple-element.11, f32[128,12,1984]{0,2,1:T(8,128)} %get-tuple-element.10, f32[128,12,1984]{0,2,1:T(8,128)} %get-tuple-element.9, f32[]{:T(128)} %bitcast.7, ...), kind=kLoop, calls=%fused_computation.14 | loop fusion | flops 69206016 | bytes 93675536 | tf_op jit(solution)/shard_map/convert_element_type | solution.py:80
  210.9 71.0 %collective-permute-done.2 = bf16[128,12,2048]{2,0,1:T(8,128)(2,1)} collective-permute-done((bf16[128,12,2048]{2,0,1:T(8,128)(2,1)}, bf16[128,12,2048]{2,0,1:T(8,128)(2,1)}, u32[]{:S(2)}, u32[]{:S(2)}) %collective-permute-start.2) | collective-permute-done | bytes 6291488 | tf_op jit(solution)/shard_map/ppermute | solution.py:25
  281.9 135.2 %collective-permute-done.1 = bf16[128,12,2048]{2,0,1:T(8,128)(2,1)} collective-permute-done((bf16[128,12,2048]{2,0,1:T(8,128)(2,1)}, bf16[128,12,2048]{2,0,1:T(8,128)(2,1)}, u32[]{:S(2)}, u32[]{:S(2)}) %collective-permute-start.1) | collective-permute-done | bytes 6291488 | tf_op jit(solution)/shard_map/ppermute | solution.py:23
  417.1 0.0 slice-done
  417.1 0.0 slice-done.1
  417.1 18.2 %pad_maximum_fusion = bf16[4,128,12,2048]{3,1,2,0:T(8,128)(2,1)} fusion(bf16[1,128,12,2048]{3,1,2,0:T(8,128)(2,1)} %bitcast.3, bf16[1,128,12,2048]{3,1,2,0:T(8,128)(2,1)S(1)} %bitcast.21, bf16[1,128,12,2048]{3,1,2,0:T(8,128)(2,1)} %bitcast.1, bf16[1,128,12,2048]{3,1,2,0:T(8,128)(2,1)} %bitcast), kind=kLoop, calls=%fused_computation.7 | loop fusion | flops 37748736 | bytes 50331648 | tf_op jit(solution)/shard_map/stack | solution.py:26
  435.3 18.7 %fusion.15 = (bf16[4,128,12,512]{3,1,2,0:T(8,128)(2,1)}, bf16[4,128,12,512]{3,1,2,0:T(8,128)(2,1)}, bf16[4,128,12,512]{3,1,2,0:T(8,128)(2,1)}, bf16[4,128,12,512]{3,1,2,0:T(8,128)(2,1)}) fusion(bf16[4,128,12,2048]{3,1,2,0:T(8,128)(2,1)} %pad_maximum_fusion), kind=kLoop, calls=%fused_computation.32 | loop fusion | bytes 50331648 | tf_op jit(solution)/shard_map/gather | solution.py:28
  454.0 6.3 %gather_fusion = bf16[4,128,12,512]{3,1,2,0:T(8,128)(2,1)} fusion(bf16[4,128,12,512]{3,1,2,0:T(8,128)(2,1)} %get-tuple-element.5, s32[1024]{0:T(1024)S(1)} %pad_clamp_fusion), kind=kCustom, calls=%fused_computation | custom fusion | bytes 12582928 | tf_op jit(solution)/shard_map/gather | solution.py:28
  460.4 6.4 %gather_fusion.1 = bf16[4,128,12,512]{3,1,2,0:T(8,128)(2,1)} fusion(bf16[4,128,12,512]{3,1,2,0:T(8,128)(2,1)} %get-tuple-element.7, s32[1024]{0:T(1024)S(1)} %pad_clamp_fusion), kind=kCustom, calls=%fused_computation.1 | custom fusion | bytes 12582928 | tf_op jit(solution)/shard_map/gather | solution.py:28
  466.8 6.5 %gather_fusion.2 = bf16[4,128,12,512]{3,1,2,0:T(8,128)(2,1)} fusion(bf16[4,128,12,512]{3,1,2,0:T(8,128)(2,1)} %get-tuple-element.6, s32[1024]{0:T(1024)S(1)} %pad_clamp_fusion), kind=kCustom, calls=%fused_computation.2 | custom fusion | bytes 12582928 | tf_op jit(solution)/shard_map/gather | solution.py:28
  473.3 6.3 %gather_fusion.3 = bf16[4,128,12,512]{3,1,2,0:T(8,128)(2,1)} fusion(bf16[4,128,12,512]{3,1,2,0:T(8,128)(2,1)} %get-tuple-element.8, s32[1024]{0:T(1024)S(1)} %pad_clamp_fusion), kind=kCustom, calls=%fused_computation.3 | custom fusion | bytes 12582928 | tf_op jit(solution)/shard_map/gather | solution.py:28
  479.6 17.4 %pad_maximum_fusion.1 = bf16[4,128,12,2048]{3,1,2,0:T(8,128)(2,1)} fusion(bf16[4,128,12,512]{3,1,2,0:T(8,128)(2,1)} %gather_fusion.3, bf16[4,128,12,512]{3,1,2,0:T(8,128)(2,1)} %gather_fusion.2, bf16[4,128,12,512]{3,1,2,0:T(8,128)(2,1)} %gather_fusion.1, bf16[4,128,12,512]{3,1,2,0:T(8,128)(2,1)} %gather_fusion), kind=kLoop, calls=%fused_computation.8 | loop fusion | flops 100663296 | bytes 50331648
  497.1 38.8 %copy.4 = bf16[4,128,12,2048]{1,0,3,2:T(4,128)(2,1)} copy(bf16[4,128,12,2048]{3,1,2,0:T(8,128)(2,1)} %pad_maximum_fusion.1) | data formatting | bytes 50331648
  535.8 17.3 %fusion = f32[512,128]{1,0:T(8,128)} fusion(bf16[128,24576]{0,1:T(8,128)(2,1)} %bitcast.22, bf16[3072,8,4,128]{3,2,1,0:T(4,128)(2,1)} %bitcast.18), kind=kOutput, calls=%fused_computation.4 | convolution fusion | flops 3221225472 | bytes 31719424 | tf_op jit(solution)/shard_map/dot_general | solution.py:56
  553.2 0.0 reduce-scatter.2.cloned.1.call-update
  553.2 33.1 %reduce-scatter.2.cloned.1.call-done = f32[64,128]{1,0:T(8,128)} async-done(((f32[512,128]{1,0:T(8,128)}), f32[64,128]{1,0:T(8,128)}) %reduce-scatter.2.cloned.1.call-update) | async-done | bytes 32784 | tf_op jit(solution)/shard_map/reduce_scatter | solution.py:82
  586.3 1.4 broadcast_multiply_fusion
  (4 shorter events, 0.0 us)
Async XLA Ops:
  6.5 17.8 %copy-start.2 = (f32[3]{0:T(128)S(1)}, f32[3]{0:T(128)}, u32[]{:S(2)}) copy-start(f32[3]{0:T(128)} %param.5) | copy-start | bytes 40
  6.5 141.8 %copy-start.1 = (s32[12,2048]{1,0:T(8,128)S(1)}, s32[12,2048]{1,0:T(8,128)}, u32[]{:S(2)}) copy-start(s32[12,2048]{1,0:T(8,128)} %param.4) | copy-start | bytes 294916
  6.5 579.7 %reduce-scatter.2.cloned.1.call-start = ((), (), s32[]{:S(2)}) async-start(), calls=%async_computation.1 | async-start | bytes 294912 | tf_op jit(solution)/shard_map/reduce_scatter | solution.py:82
  6.5 141.8 %collective-permute-start = (bf16[128,12,2048]{2,0,1:T(8,128)(2,1)}, bf16[128,12,2048]{2,0,1:T(8,128)(2,1)}, u32[]{:S(2)}, u32[]{:S(2)}) collective-permute-start(bf16[128,12,2048]{2,0,1:T(8,128)(2,1)} %param.3), channel_id=1, source_target_pairs={{0,1},{1,2},{2,3},{3,0},{4,5},{5,6},{6,7},{7,4},{8,9},{9,10},{10,1... | collective-permute-start | bytes 18874376 | tf_op jit(solution)/shard_map/ppermute | solution.py:23
  9.6 272.3 %collective-permute-start.2 = (bf16[128,12,2048]{2,0,1:T(8,128)(2,1)}, bf16[128,12,2048]{2,0,1:T(8,128)(2,1)}, u32[]{:S(2)}, u32[]{:S(2)}) collective-permute-start(bf16[128,12,2048]{2,0,1:T(8,128)(2,1)} %param.3), channel_id=1, source_target_pairs={{1,0},{2,1},{3,2},{0,3},{5,4},{6,5},{7,6},{4,7},{9,8},{10,9},{11,1... | collective-permute-start | bytes 18874376 | tf_op jit(solution)/shard_map/ppermute | solution.py:25
  21.5 127.4 %collective-permute-start.3 = (bf16[128,1,2048]{0,2,1:T(8,128)(2,1)S(1)}, bf16[128,1,2048]{0,2,1:T(8,128)(2,1)S(1)}, u32[]{:S(2)}, u32[]{:S(2)}) collective-permute-start(bf16[128,1,2048]{0,2,1:T(8,128)(2,1)S(1)} %get-tuple-element.13), channel_id=1, source_target_pairs={{0,4},{4,8},{8,12},{12,16},{16,20},{20,24},{24,28},{1,5},{5,9},{9,... | collective-permute-start | bytes 1572872 | tf_op jit(solution)/shard_map/ppermute | solution.py:39
  23.0 125.9 %collective-permute-start.4 = (bf16[128,1,2048]{0,2,1:T(8,128)(2,1)S(1)}, bf16[128,1,2048]{0,2,1:T(8,128)(2,1)S(1)}, u32[]{:S(2)}, u32[]{:S(2)}) collective-permute-start(bf16[128,1,2048]{0,2,1:T(8,128)(2,1)S(1)} %get-tuple-element.14), channel_id=1, source_target_pairs={{4,0},{8,4},{12,8},{16,12},{20,16},{24,20},{28,24},{5,1},{9,5},{13... | collective-permute-start | bytes 1572872 | tf_op jit(solution)/shard_map/ppermute | solution.py:40
  148.3 268.8 %collective-permute-start.1 = (bf16[128,12,2048]{2,0,1:T(8,128)(2,1)}, bf16[128,12,2048]{2,0,1:T(8,128)(2,1)}, u32[]{:S(2)}, u32[]{:S(2)}) collective-permute-start(bf16[128,12,2048]{2,0,1:T(8,128)(2,1)} %collective-permute-done), channel_id=1, source_target_pairs={{0,1},{1,2},{2,3},{3,0},{4,5},{5,6},{6,7},{7,4},{8,9},{9,10},{10,1... | collective-permute-start | bytes 18874376 | tf_op jit(solution)/shard_map/ppermute | solution.py:23
  158.1 20.0 %copy-start = (f32[128,14,2048]{0,2,1:T(8,128)S(1)}, f32[128,14,2048]{0,2,1:T(8,128)}, u32[]{:S(2)}) copy-start(f32[128,14,2048]{0,2,1:T(8,128)} %maximum_convert_fusion) | copy-start | bytes 44040196
  178.1 239.0 %slice-start = ((s8[6291456]{0:T(1024)(128)(4,1)}), s8[4194304]{0:T(1024)(128)(4,1)S(1)}, s32[]{:S(2)}) async-start(s8[6291456]{0:T(1024)(128)(4,1)} %bitcast.19), calls=%async_computation.2 | async-start | bytes 8388608
  187.1 230.0 %slice-start.1 = ((s8[6291456]{0:T(1024)(128)(4,1)}), s8[2097152]{0:T(1024)(128)(4,1)S(1)}, s32[]{:S(2)}) async-start(s8[6291456]{0:T(1024)(128)(4,1)} %bitcast.19), calls=%async_computation.3 | async-start | bytes 4194304
Sparse Core Ops, SparseCore 0:
  553.3 32.9 reduce-scatter.1
